TPU v7x, 256 devices: a whole 4x4x8 slice. The times are simulated.
256 devices in a mesh: rep: 2 (over core), exp: 128 (over x, y, z).
Axes of the slice: x: 4, y: 4, z: 8, core: 2. Of those that a mesh axis runs over, the one named last changes fastest.
Arguments:
- attn_out: bfloat16 [16384, 4096], P(('rep', 'exp')), may hold values from -6 to 6
- out_weight: bfloat16 [4096, 2048], P('exp'), may hold values from -0.09375 to 0.09375
- router_weight: bfloat16 [2048, 128], replicated, may hold values from -0.125 to 0.125
- gate_weight: bfloat16 [128, 2048, 768], P('exp'), may hold values from -0.125 to 0.125
- up_weight: bfloat16 [128, 2048, 768], P('exp'), may hold values from -0.125 to 0.125
- down_weight: bfloat16 [128, 768, 2048], P('exp'), may hold values from -0.21875 to 0.21875
- cotangent: bfloat16 [16384, 2048], P(('rep', 'exp')), may hold values from -6 to 6
- log_ratios: float32 [16384], P(('rep', 'exp')), may hold values from -0.03 to 0.05
- expert_ids: int32 [16384, 8], P(('rep', 'exp')), may hold values from 0 to 127, as said below
- slot_ids: int32 [16384, 8], P(('rep', 'exp')), may hold values from 0 to 5, as said below
- episode_ids: int32 [16384], P(('rep', 'exp')), may hold values from 0 to 255, never falling along the last dimension, each value on 1 to 256 neighbouring positions
Outputs:
- token_grads: bfloat16 [16384, 4096], P(('rep', 'exp'))
- router_grad: float32 [2048, 128], P('exp')
Inputs may be any that keep to these rules, and one draw needn't show every extreme that they name: `expert_ids`: each row names 8 different experts. Among the rows of one device no expert is named more than 6 times, and on every device some expert is named exactly 6 times. `slot_ids`: among the rows of one device, the pairs of a row with one expert named in it get distinct slots; the slots of one expert on one device are 0 up to the number of its pairs there minus 1. `episode_ids`: episodes are runs of consecutive tokens, numbered in order; each has 1 to 256 tokens, one exactly 256.
All inputs are finite; a program needn't handle non-finite values.
Results may differ from a plain program's by a relative error of at most 0.012.
Values may be sent and summed in bfloat16 or wider, within the bound.
No kernel may reach another device: no remote copies, remote signals or barrier semaphores. Data moves between devices by JAX's collectives and lax.ppermute only.
A program may use at most 128 MiB of HBM per device.

v0:
```python
import jax
import jax.numpy as jnp
from jax import lax
from jax.sharding import PartitionSpec as P

clip_top = 4.0


def shards(
    attn_out,
    out_weight,
    router_weight,
    gate_weight,
    up_weight,
    down_weight,
    cotangent,
    log_ratios,
    expert_ids,
    slot_ids,
    episode_ids,
):
    tok_count = attn_out.shape[0]
    top_count = expert_ids.shape[1]
    model_width = cotangent.shape[1]
    expert_count = lax.axis_size("exp")
    device_count = lax.axis_size("rep") * expert_count
    capacity = 3 * tok_count * top_count // (2 * expert_count)
    episode_count = tok_count * device_count // 64
    episode_hits = (
        episode_ids[:, None] == jnp.arange(episode_count, dtype=jnp.int32)[None, :]
    ).astype(jnp.float32)
    part_logs = jnp.sum(episode_hits * log_ratios[:, None], axis=0)
    part_counts = jnp.sum(episode_hits, axis=0)
    log_sums, counts = lax.psum((part_logs, part_counts), ("rep", "exp"))
    episode_weight = jnp.minimum(jnp.exp(log_sums), clip_top)
    mean_weight = jnp.sum(counts * episode_weight) / (tok_count * device_count)
    token_scale = jnp.sum(episode_hits * episode_weight[None, :], axis=1) / mean_weight
    weight_full = lax.all_gather(out_weight, "exp", axis=0, tiled=True)
    hidden = jnp.dot(attn_out, weight_full, preferred_element_type=jnp.float32).astype(jnp.bfloat16)
    logits = jnp.dot(hidden, router_weight, preferred_element_type=jnp.float32)
    expert_hits = (expert_ids[:, :, None] == jnp.arange(expert_count, dtype=jnp.int32)).astype(
        jnp.float32
    )
    chosen = jnp.sum(expert_hits * logits[:, None, :], axis=2)
    raised = jnp.exp(chosen)
    gate_probs = raised / jnp.sum(raised, axis=1, keepdims=True)
    targets = expert_ids * capacity + slot_ids
    slot_count = expert_count * capacity
    labels = jnp.arange(tok_count, dtype=jnp.int32)[:, None] + 1
    matches = (targets[:, :, None] == jnp.arange(slot_count, dtype=jnp.int32)).astype(jnp.int32)
    owners = jnp.sum(matches * labels[:, :, None], axis=(0, 1))
    filled = owners > 0
    source_rows = jnp.maximum(owners - 1, 0)
    zero_value = jnp.zeros((), jnp.bfloat16)
    send_hidden = jnp.where(filled[:, None], hidden[source_rows], zero_value).reshape(
        expert_count, capacity, model_width
    )
    send_cot = jnp.where(filled[:, None], cotangent[source_rows], zero_value).reshape(
        expert_count, capacity, model_width
    )
    rows_in = lax.all_to_all(send_hidden, "exp", split_axis=0, concat_axis=0, tiled=True)
    cot_in = lax.all_to_all(send_cot, "exp", split_axis=0, concat_axis=0, tiled=True)
    gate_pre = jnp.einsum(
        "snd,df->snf", rows_in, gate_weight[0], preferred_element_type=jnp.float32
    )
    up_pre = jnp.einsum("snd,df->snf", rows_in, up_weight[0], preferred_element_type=jnp.float32)
    upstream = jnp.einsum("snd,fd->snf", cot_in, down_weight[0], preferred_element_type=jnp.float32)
    sigmoid_gate = jax.nn.sigmoid(gate_pre)
    slot_score = jnp.sum(upstream * (gate_pre * sigmoid_gate * up_pre), axis=2)
    grad_gate = (upstream * up_pre * sigmoid_gate * (1.0 + gate_pre * (1.0 - sigmoid_gate))).astype(
        jnp.bfloat16
    )
    grad_up = (upstream * gate_pre * sigmoid_gate).astype(jnp.bfloat16)
    back_rows = (
        jnp.einsum("snf,df->snd", grad_gate, gate_weight[0], preferred_element_type=jnp.float32)
        + jnp.einsum("snf,df->snd", grad_up, up_weight[0], preferred_element_type=jnp.float32)
    ).astype(jnp.bfloat16)
    back_home = lax.all_to_all(back_rows, "exp", split_axis=0, concat_axis=0, tiled=True)
    score_home = lax.all_to_all(slot_score, "exp", split_axis=0, concat_axis=0, tiled=True)
    pair_back = back_home.reshape(slot_count, model_width)[targets]
    pair_score = score_home.reshape(slot_count)[targets]
    mixed_back = jnp.sum(gate_probs[:, :, None] * pair_back.astype(jnp.float32), axis=1)
    logit_grad = gate_probs * (pair_score - jnp.sum(gate_probs * pair_score, axis=1, keepdims=True))
    full_grad = jnp.sum(expert_hits * logit_grad[:, :, None], axis=1)
    weighted = (token_scale[:, None] * full_grad).astype(jnp.bfloat16)
    router_part = jnp.einsum("td,te->de", hidden, weighted, preferred_element_type=jnp.float32)
    grad_hidden = (
        token_scale[:, None] * mixed_back
        + jnp.dot(weighted, router_weight.T, preferred_element_type=jnp.float32)
    ).astype(jnp.bfloat16)
    token_grads = jnp.dot(grad_hidden, weight_full.T, preferred_element_type=jnp.float32).astype(
        jnp.bfloat16
    )
    router_total = lax.psum(router_part, ("rep", "exp"))
    row_count = model_width // expert_count
    router_grad = lax.dynamic_slice_in_dim(
        router_total, lax.axis_index("exp") * row_count, row_count, 0
    )
    return (token_grads, router_grad)


def solution(mesh):
    placed = (
        P(("rep", "exp"), None),
        P("exp", None),
        P(),
        P("exp", None, None),
        P("exp", None, None),
        P("exp", None, None),
        P(("rep", "exp"), None),
        P(("rep", "exp")),
        P(("rep", "exp"), None),
        P(("rep", "exp"), None),
        P(("rep", "exp")),
    )
    return jax.shard_map(
        shards,
        mesh=mesh,
        in_specs=placed,
        out_specs=(P(("rep", "exp"), None), P("exp", None)),
        check_vma=False,
    )
```

profile of v0, /device:TPU:2, one launch (start us, length us, event | category | flops | bytes accessed | tf_op | source)
XLA Modules:
  0.0 948.8 jit_solution(6600559267684554942)
XLA Ops:
  9.3 4.3 gather_fusion
  13.5 6.3 gather.17
  19.8 144.6 %all-gather.2.cloned.1.call-done = bf16[4096,2048]{1,0:T(8,128)(2,1)} async-done(((bf16[32,2048]{1,0:T(8,128)(2,1)}), bf16[4096,2048]{1,0:T(8,128)(2,1)}) %all-gather.2.cloned.1.call-update) | async-done | bytes 16777232 | tf_op jit(solution)/shard_map/all_gather | solution.py:38
  164.4 9.0 convolution_convert_fusion.1
  173.4 4.3 gather_fusion.1
  177.7 6.2 gather.19
  184.0 5.2 broadcast_select_fusion.1
  189.2 106.0 %all_to_all.24 = bf16[128,6,2048]{2,1,0:T(8,128)(2,1)} all-to-all(bf16[128,6,2048]{2,1,0:T(8,128)(2,1)S(1)} %get-tuple-element.9), channel_id=1, replica_groups=mesh['rep'=2,'exp'=128] {'exp'}, dimensions={0} | all-to-all | bytes 6291456 | tf_op jit(solution)/shard_map/all_to_all | solution.py:61
  295.2 10.3 %all-to-all-start = ((bf16[128,6,2048]{2,1,0:T(8,128)(2,1)}), bf16[128,6,2048]{2,1,0:T(8,128)(2,1)}, u32[]{:S(2)}, u32[]{:S(2)}) async-start(bf16[128,6,2048]{2,1,0:T(8,128)(2,1)} %get-tuple-element.8), calls=%async_computation | async-start | bytes 8388608 | tf_op jit(solution)/shard_map/all_to_all | solution.py:62
  305.6 9.3 fusion.3
  314.9 7.5 fusion.6
  322.4 76.0 %all-to-all-done = bf16[128,6,2048]{2,1,0:T(8,128)(2,1)} async-done(((bf16[128,6,2048]{2,1,0:T(8,128)(2,1)}), bf16[128,6,2048]{2,1,0:T(8,128)(2,1)}, u32[]{:S(2)}, u32[]{:S(2)}) %all-to-all-start) | async-done | bytes 3145760 | tf_op jit(solution)/shard_map/all_to_all | solution.py:62
  398.5 11.8 %multiply_reduce_fusion = (f32[128,6]{0,1:T(8,128)S(1)}, f32[128,6,768]{2,0,1:T(8,128)}) fusion(f32[128,6,768]{2,0,1:T(8,128)} %fusion.6, f32[128,6,768]{2,0,1:T(8,128)} %fusion.3, bf16[1,768,2048]{2,1,0:T(8,128)(2,1)} %param.16, bf16[128,6,2048]{2,1,0:T(8,128)(2,1)} %all-to-all-done), kind=kOutput, calls=%fused_computation.20 | convolution fusion | flops 2420047104 | bytes 13372416 | tf_op jit(solution)/shard_map/snd,fd->snf/dot_general | solution.py:67
  411.1 8.7 all-to-all-start.3
  419.8 5.6 fusion.1
  428.3 3.7 copy.35
  432.1 14.4 %all-to-all-start.2 = ((bf16[128,6,2048]{2,1,0:T(8,128)(2,1)}), bf16[128,6,2048]{2,1,0:T(8,128)(2,1)}, u32[]{:S(2)}, u32[]{:S(2)}) async-start(bf16[128,6,2048]{2,1,0:T(8,128)(2,1)} %copy.35), calls=%async_computation.2 | async-start | bytes 8388608 | tf_op jit(solution)/shard_map/all_to_all | solution.py:78
  446.9 130.2 %psum.21 = f32[256]{0:T(256)S(1)} all-reduce(f32[256]{0:T(256)S(1)} %select_reduce_fusion.4), channel_id=1, replica_groups=mesh['rep'=2,'exp'=128] {'rep','exp'}, use_global_device_ids=true, to_apply=%region_1.0 | all-reduce | flops 256 | bytes 2048 | tf_op jit(solution)/shard_map/psum | solution.py:34
  577.3 74.9 %psum.22 = f32[256]{0:T(256)S(1)} all-reduce(f32[256]{0:T(256)S(1)} %get-tuple-element.2), channel_id=1, replica_groups=mesh['rep'=2,'exp'=128] {'rep','exp'}, use_global_device_ids=true, to_apply=%region_4.0 | all-reduce | flops 256 | bytes 2048 | tf_op jit(solution)/shard_map/psum | solution.py:34
  659.8 255.7 %all-reduce.2.cloned.1.call-done = f32[2048,128]{1,0:T(8,128)} async-done(((f32[2048,128]{1,0:T(8,128)}), f32[2048,128]{1,0:T(8,128)}) %all-reduce.2.cloned.1.call-update) | async-done | bytes 1048592 | tf_op jit(solution)/shard_map/psum | solution.py:94
  916.8 4.9 reshape.115
  921.7 3.3 gather_fusion.2
  925.0 4.2 fusion
  929.2 12.5 %convolution_convert_fusion = bf16[64,4096]{1,0:T(8,128)(2,1)} fusion(bf16[4096,2048]{1,0:T(8,128)(2,1)} %all-gather.2.cloned.1.call-done, bf16[2048,128]{1,0:T(8,128)(2,1)} %param.13, f32[64,2048]{1,0:T(8,128)} %fusion, f32[64]{0:T(128)S(1)} %broadcast_divide_fusion, f32[64,128]{1,0:T(8,128)S(1)} %select_reduce_fusion.1), kind=kOutput, calls=%fused_computation.5 | convolution fusion | flops 1107968000 | bytes 18383104 | tf_op jit(solution)/shard_map/dot_general | solution.py:91
  (62 shorter events, 14.4 us)
Async XLA Ops:
  7.2 298.4 %copy-start = (bf16[1,2048,768]{2,1,0:T(8,128)(2,1)S(1)}, bf16[1,2048,768]{2,1,0:T(8,128)(2,1)}, u32[]{:S(2)}) copy-start(bf16[1,2048,768]{2,1,0:T(8,128)(2,1)} %param.14) | copy-start | bytes 9437188
  7.2 2.1 copy-start.2
  7.2 157.2 %all-gather.2.cloned.1.call-start = ((), (), s32[]{:S(2)}) async-start(), calls=%async_computation.4 | async-start | bytes 16908288 | tf_op jit(solution)/shard_map/all_gather | solution.py:38
  295.2 103.3 %all-to-all-start = ((bf16[128,6,2048]{2,1,0:T(8,128)(2,1)}), bf16[128,6,2048]{2,1,0:T(8,128)(2,1)}, u32[]{:S(2)}, u32[]{:S(2)}) async-start(bf16[128,6,2048]{2,1,0:T(8,128)(2,1)} %get-tuple-element.8), calls=%async_computation | async-start | bytes 8388608 | tf_op jit(solution)/shard_map/all_to_all | solution.py:62
  305.5 9.4 copy-start.3
  305.5 9.4 copy-start.8
  411.1 21.0 %all-to-all-start.3 = ((f32[128,1,6]{2,1,0:T(1,128)}), f32[128,1,6]{2,1,0:T(1,128)S(1)}, u32[]{:S(2)}, u32[]{:S(2)}) async-start(f32[128,1,6]{2,1,0:T(1,128)} %copy.37), calls=%async_computation.3 | async-start | bytes 131072 | tf_op jit(solution)/shard_map/all_to_all | solution.py:79
  419.8 5.6 copy-start.9
  419.8 5.6 copy-start.10
  419.8 5.6 copy-start.11
  432.0 14.5 %copy-start.5 = (s32[64,8]{0,1:T(8,128)S(1)}, s32[64,8]{0,1:T(8,128)}, u32[]{:S(2)}) copy-start(s32[64,8]{0,1:T(8,128)} %param.19) | copy-start | bytes 6148
  432.0 14.8 %copy-start.6 = (s32[64]{0:T(128)S(1)}, s32[64]{0:T(128)}, u32[]{:S(2)}) copy-start(s32[64]{0:T(128)} %param.21) | copy-start | bytes 772
  432.0 14.8 %copy-start.7 = (f32[64]{0:T(128)S(1)}, f32[64]{0:T(128)}, u32[]{:S(2)}) copy-start(f32[64]{0:T(128)} %param.18) | copy-start | bytes 772
  432.1 221.4 %copy-start.4 = (bf16[2048,128]{1,0:T(8,128)(2,1)S(1)}, bf16[2048,128]{1,0:T(8,128)(2,1)}, u32[]{:S(2)}) copy-start(bf16[2048,128]{1,0:T(8,128)(2,1)} %param.13) | copy-start | bytes 1572868
  432.1 484.7 %all-to-all-start.2 = ((bf16[128,6,2048]{2,1,0:T(8,128)(2,1)}), bf16[128,6,2048]{2,1,0:T(8,128)(2,1)}, u32[]{:S(2)}, u32[]{:S(2)}) async-start(bf16[128,6,2048]{2,1,0:T(8,128)(2,1)} %copy.35), calls=%async_computation.2 | async-start | bytes 8388608 | tf_op jit(solution)/shard_map/all_to_all | solution.py:78
  446.5 469.0 %all-reduce.2.cloned.1.call-start = ((), (), s32[]{:S(2)}) async-start(), calls=%async_computation.5 | async-start | bytes 2097152 | tf_op jit(solution)/shard_map/psum | solution.py:94
  929.2 12.5 %copy-start.1 = (bf16[1,2048,768]{2,1,0:T(8,128)(2,1)S(1)}, bf16[1,2048,768]{2,1,0:T(8,128)(2,1)}, u32[]{:S(2)}) copy-start(bf16[1,2048,768]{2,1,0:T(8,128)(2,1)} %param.14) | copy-start | bytes 9437188
Sparse Core Ops, SparseCore 0:
  11.6 152.7 all-gather.1
  659.9 255.5 all-reduce.1
where the time goes:
time: 957 us; the launch traced here: 949 us
  waiting for transfers between devices  477 us (50%)
  blocking collectives  311 us (32%)
  matrix products  60.2 us (6%)
  local copies, waits for them, and re-layouts  38.7 us (4%)
  starting transfers between devices  33.5 us (4%)
  between operations  15.2 us (2%)
  other arithmetic  13 us (1%)
    psum x1, waiting for transfers between devices, shards(): router_total = lax.psum(router_part, ('rep', 'exp'))  256 us
    psum x2, blocking collectives, shards(): log_sums, counts = lax.psum((part_logs, part_counts), ('rep', 'exp'))  205 us
    all_gather x1, waiting for transfers between devices, shards(): weight_full = lax.all_gather(out_weight, 'exp', axis=0, tiled=True)  145 us
    all_to_all x1, blocking collectives, shards(): lax.all_to_all(send_hidden, 'exp', split_axis=0, concat_axis=0, tiled=True)  106 us
    all_to_all x1, waiting for transfers between devices, shards(): lax.all_to_all(send_cot, 'exp', split_axis=0, concat_axis=0, tiled=True)  76 us
  transfers between devices with their start and end apart: 5, of which 3 were waited for; matrix products, arithmetic and copies ran while one was open for 5% of the time, Pallas kernels for 0%

commit v1 on v0

--- a/solution.py
+++ b/solution.py
@@ -35,7 +35,9 @@
     episode_weight = jnp.minimum(jnp.exp(log_sums), clip_top)
     mean_weight = jnp.sum(counts * episode_weight) / (tok_count * device_count)
     token_scale = jnp.sum(episode_hits * episode_weight[None, :], axis=1) / mean_weight
-    weight_full = lax.all_gather(out_weight, "exp", axis=0, tiled=True)
+    weight_full = jnp.concatenate(
+        lax.all_to_all(jnp.stack([out_weight] * lax.axis_size("exp")), "exp", 0, 0), axis=0
+    )
     hidden = jnp.dot(attn_out, weight_full, preferred_element_type=jnp.float32).astype(jnp.bfloat16)
     logits = jnp.dot(hidden, router_weight, preferred_element_type=jnp.float32)
     expert_hits = (expert_ids[:, :, None] == jnp.arange(expert_count, dtype=jnp.int32)).astype(

time: 957 us -> 1210 us (1.26)
  waiting for transfers between devices: 477 us -> 686 us
  starting transfers between devices: 33.5 us -> 49.1 us
  local copies, waits for them, and re-layouts: 38.7 us -> 53.2 us
    all_to_all x0 -> x1, waiting for transfers between devices: none -> 353 us  [shards(): lax.all_to_all(jnp.stack([out_weight] * lax.axis_size('exp')), 'exp', 0, 0)]
    all_gather x1 -> x0, waiting for transfers between devices: 145 us -> none  [shards(): weight_full = lax.all_gather(out_weight, 'exp', axis=0, tiled=True)]
    all_to_all x0 -> x1, starting transfers between devices: none -> 16.1 us  [shards(): lax.all_to_all(jnp.stack([out_weight] * lax.axis_size('exp')), 'exp', 0, 0)]
  transfers between devices with their start and end apart: 5 -> 5, of which waited for: 3 -> 3; matrix products, arithmetic and copies ran while one was open for 5% -> 4% of each run, Pallas kernels for 0% -> 0%
where the time goes in v1:
time: 1210 us; the launch traced here: 1200 us
  waiting for transfers between devices  686 us (57%)
  blocking collectives  317 us (26%)
  matrix products  61.2 us (5%)
  local copies, waits for them, and re-layouts  53.2 us (4%)
  starting transfers between devices  49.1 us (4%)
  between operations  15.1 us (1%)
  other arithmetic  13.7 us (1%)
    all_to_all x1, waiting for transfers between devices, shards(): lax.all_to_all(jnp.stack([out_weight] * lax.axis_size('exp')), 'exp', 0, 0)  353 us
    psum x1, waiting for transfers between devices, shards(): router_total = lax.psum(router_part, ('rep', 'exp'))  256 us
    psum x2, blocking collectives, shards(): log_sums, counts = lax.psum((part_logs, part_counts), ('rep', 'exp'))  205 us
    all_to_all x1, blocking collectives, shards(): lax.all_to_all(send_hidden, 'exp', split_axis=0, concat_axis=0, tiled=True)  112 us
    all_to_all x1, waiting for transfers between devices, shards(): lax.all_to_all(send_cot, 'exp', split_axis=0, concat_axis=0, tiled=True)  77.2 us
  transfers between devices with their start and end apart: 5, of which 3 were waited for; matrix products, arithmetic and copies ran while one was open for 4% of the time, Pallas kernels for 0%

profile of v1, /device:TPU:2, one launch (start us, length us, event | category | flops | bytes accessed | tf_op | source)
XLA Modules:
  0.0 1195.7 jit_solution(7333654830277722228)
XLA Ops:
  7.2 6.9 stack.2
  14.1 16.1 %all-to-all-start = ((bf16[128,32,2048]{2,1,0:T(8,128)(2,1)}), bf16[128,32,2048]{2,1,0:T(8,128)(2,1)}, u32[]{:S(2)}, u32[]{:S(2)}) async-start(bf16[128,32,2048]{2,1,0:T(8,128)(2,1)} %stack.2), calls=%async_computation | async-start | bytes 33554432 | tf_op jit(solution)/shard_map/all_to_all | solution.py:39
  30.6 4.3 gather_fusion
  34.9 6.2 gather.17
  41.3 353.3 %all-to-all-done = bf16[128,32,2048]{2,1,0:T(8,128)(2,1)} async-done(((bf16[128,32,2048]{2,1,0:T(8,128)(2,1)}), bf16[128,32,2048]{2,1,0:T(8,128)(2,1)}, u32[]{:S(2)}, u32[]{:S(2)}) %all-to-all-start) | async-done | bytes 16777248 | tf_op jit(solution)/shard_map/all_to_all | solution.py:39
  394.6 9.0 convolution_convert_fusion.1
  403.6 4.3 gather_fusion.1
  407.9 6.2 gather.19
  414.1 5.3 broadcast_select_fusion.1
  419.4 112.2 %all_to_all.29 = bf16[128,6,2048]{2,1,0:T(8,128)(2,1)} all-to-all(bf16[128,6,2048]{2,1,0:T(8,128)(2,1)S(1)} %get-tuple-element.9), channel_id=1, replica_groups=mesh['rep'=2,'exp'=128] {'exp'}, dimensions={0} | all-to-all | bytes 6291456 | tf_op jit(solution)/shard_map/all_to_all | solution.py:63
  531.6 10.0 all-to-all-start.1
  541.6 9.4 fusion.3
  551.0 7.5 fusion.6
  558.5 77.2 %all-to-all-done.1 = bf16[128,6,2048]{2,1,0:T(8,128)(2,1)} async-done(((bf16[128,6,2048]{2,1,0:T(8,128)(2,1)}), bf16[128,6,2048]{2,1,0:T(8,128)(2,1)}, u32[]{:S(2)}, u32[]{:S(2)}) %all-to-all-start.1) | async-done | bytes 3145760 | tf_op jit(solution)/shard_map/all_to_all | solution.py:64
  635.7 11.9 multiply_reduce_fusion
  648.3 8.7 all-to-all-start.4
  657.0 5.6 fusion.1
  669.9 14.3 %all-to-all-start.3 = ((bf16[128,6,2048]{2,1,0:T(8,128)(2,1)}), bf16[128,6,2048]{2,1,0:T(8,128)(2,1)}, u32[]{:S(2)}, u32[]{:S(2)}) async-start(bf16[128,6,2048]{2,1,0:T(8,128)(2,1)} %copy.35), calls=%async_computation.3 | async-start | bytes 8388608 | tf_op jit(solution)/shard_map/all_to_all | solution.py:80
  684.6 130.9 %psum.21 = f32[256]{0:T(256)S(1)} all-reduce(f32[256]{0:T(256)S(1)} %select_reduce_fusion.4), channel_id=1, replica_groups=mesh['rep'=2,'exp'=128] {'rep','exp'}, use_global_device_ids=true, to_apply=%region_1.0 | all-reduce | flops 256 | bytes 2048 | tf_op jit(solution)/shard_map/psum | solution.py:34
  815.7 74.1 %psum.22 = f32[256]{0:T(256)S(1)} all-reduce(f32[256]{0:T(256)S(1)} %get-tuple-element.2), channel_id=1, replica_groups=mesh['rep'=2,'exp'=128] {'rep','exp'}, use_global_device_ids=true, to_apply=%region_4.0 | all-reduce | flops 256 | bytes 2048 | tf_op jit(solution)/shard_map/psum | solution.py:34
  901.3 255.7 %all-reduce.2.cloned.1.call-done = f32[2048,128]{1,0:T(8,128)} async-done(((f32[2048,128]{1,0:T(8,128)}), f32[2048,128]{1,0:T(8,128)}) %all-reduce.2.cloned.1.call-update) | async-done | bytes 1048592 | tf_op jit(solution)/shard_map/psum | solution.py:96
  1158.3 6.3 reshape.121
  1164.6 7.6 gather_fusion.2
  1176.4 12.3 %convolution_convert_fusion = bf16[64,4096]{1,0:T(8,128)(2,1)} fusion(bf16[4096,2048]{1,0:T(8,128)(2,1)} %bitcast, bf16[2048,128]{1,0:T(8,128)(2,1)} %param.13, f32[64,2048]{1,0:T(8,128)} %fusion, f32[64]{0:T(128)S(1)} %broadcast_divide_fusion, f32[64,128]{1,0:T(8,128)S(1)} %select_reduce_fusion.1), kind=kOutput, calls=%fused_computation.5 | convolution fusion | flops 1107968000 | bytes 18383104 | tf_op jit(solution)/shard_map/dot_general | solution.py:93
  (66 shorter events, 25.4 us)
Async XLA Ops:
  7.2 534.4 %copy-start = (bf16[1,2048,768]{2,1,0:T(8,128)(2,1)S(1)}, bf16[1,2048,768]{2,1,0:T(8,128)(2,1)}, u32[]{:S(2)}) copy-start(bf16[1,2048,768]{2,1,0:T(8,128)(2,1)} %param.14) | copy-start | bytes 9437188
  14.1 16.2 %copy-start.6 = (s32[64,8]{0,1:T(8,128)S(1)}, s32[64,8]{0,1:T(8,128)}, u32[]{:S(2)}) copy-start(s32[64,8]{0,1:T(8,128)} %param.19) | copy-start | bytes 6148
  14.1 16.2 %copy-start.7 = (s32[64,8]{0,1:T(8,128)S(1)}, s32[64,8]{0,1:T(8,128)}, u32[]{:S(2)}) copy-start(s32[64,8]{0,1:T(8,128)} %param.20) | copy-start | bytes 6148
  14.1 16.5 %copy-start.1 = (bf16[64,2048]{1,0:T(8,128)(2,1)S(1)}, bf16[64,2048]{1,0:T(8,128)(2,1)}, u32[]{:S(2)}) copy-start(bf16[64,2048]{1,0:T(8,128)(2,1)} %param.17) | copy-start | bytes 786436
  14.1 380.5 %all-to-all-start = ((bf16[128,32,2048]{2,1,0:T(8,128)(2,1)}), bf16[128,32,2048]{2,1,0:T(8,128)(2,1)}, u32[]{:S(2)}, u32[]{:S(2)}) async-start(bf16[128,32,2048]{2,1,0:T(8,128)(2,1)} %stack.2), calls=%async_computation | async-start | bytes 33554432 | tf_op jit(solution)/shard_map/all_to_all | solution.py:39
  531.6 104.1 %all-to-all-start.1 = ((bf16[128,6,2048]{2,1,0:T(8,128)(2,1)}), bf16[128,6,2048]{2,1,0:T(8,128)(2,1)}, u32[]{:S(2)}, u32[]{:S(2)}) async-start(bf16[128,6,2048]{2,1,0:T(8,128)(2,1)} %get-tuple-element.8), calls=%async_computation.1 | async-start | bytes 8388608 | tf_op jit(solution)/shard_map/all_to_all | solution.py:64
  541.6 9.4 copy-start.2
  541.6 9.4 copy-start.10
  648.3 21.0 %all-to-all-start.4 = ((f32[128,1,6]{2,1,0:T(1,128)}), f32[128,1,6]{2,1,0:T(1,128)S(1)}, u32[]{:S(2)}, u32[]{:S(2)}) async-start(f32[128,1,6]{2,1,0:T(1,128)} %copy.37), calls=%async_computation.4 | async-start | bytes 131072 | tf_op jit(solution)/shard_map/all_to_all | solution.py:81
  657.0 5.6 copy-start.11
  657.0 5.6 copy-start.12
  657.0 5.6 copy-start.13
  669.3 15.2 %copy-start.8 = (s32[64]{0:T(128)S(1)}, s32[64]{0:T(128)}, u32[]{:S(2)}) copy-start(s32[64]{0:T(128)} %param.21) | copy-start | bytes 772
  669.3 15.2 %copy-start.9 = (f32[64]{0:T(128)S(1)}, f32[64]{0:T(128)}, u32[]{:S(2)}) copy-start(f32[64]{0:T(128)} %param.18) | copy-start | bytes 772
  669.3 0.6 copy-start.5
  669.9 488.3 %all-to-all-start.3 = ((bf16[128,6,2048]{2,1,0:T(8,128)(2,1)}), bf16[128,6,2048]{2,1,0:T(8,128)(2,1)}, u32[]{:S(2)}, u32[]{:S(2)}) async-start(bf16[128,6,2048]{2,1,0:T(8,128)(2,1)} %copy.35), calls=%async_computation.3 | async-start | bytes 8388608 | tf_op jit(solution)/shard_map/all_to_all | solution.py:80
  684.2 472.8 %all-reduce.2.cloned.1.call-start = ((), (), s32[]{:S(2)}) async-start(), calls=%async_computation.5 | async-start | bytes 2097152 | tf_op jit(solution)/shard_map/psum | solution.py:96
  899.0 0.6 copy-start.3
  1164.6 7.6 copy-start.4
Sparse Core Ops, SparseCore 0:
  901.4 255.4 all-reduce.1
